TPU v7x, 32 devices: a whole 2x2x4 slice. The times are simulated.
32 devices in a mesh: gx: 4 (over y, core), gy: 8 (over z, x).
Axes of the slice: x: 2, y: 2, z: 4, core: 2. Of those that a mesh axis runs over, the one named last changes fastest.
Arguments:
- points: bfloat16 [32768, 64], P(('gx', 'gy')), may hold values from -25 to 25
- solution: float32 [32768, 32], P(('gx', 'gy')), may hold values from -6 to 6
- residual: float32 [32768, 32], P(('gx', 'gy')), may hold values from -36 to 36
- near_leaves: int32 [64, 4], P(('gx', 'gy')), may hold values from 0 to 63, as said below
- node_skeleton: int32 [32, 128], P(('gx', 'gy')), may hold values from 0 to 1023, as said below
- upper_skeleton: int32 [31, 128], replicated, may hold values from 0 to 255, as said below
- far_nodes: int32 [64, 16], P(('gx', 'gy')), may hold values from 0 to 62, as said below
Outputs:
- solution_next: float32 [32768, 32], P(('gx', 'gy'))
- residual_next: float32 [32768, 32], P(('gx', 'gy'))
- matvec_image: float32 [32768, 32], P(('gx', 'gy'))
Inputs may be any that keep to these rules, and one draw needn't show every extreme that they name: `near_leaves`: leaves are numbered in point order, 2 to a device in the flat device order. A leaf's 4 near leaves are distinct and lie on other devices of its gx row; the near leaves named by one device's leaves are all distinct, at most 2 of them lie on any one other device, and exactly 2 on some. `node_skeleton`: each row holds 128 distinct positions among its device's 1024 points. `upper_skeleton`: row u holds 128 distinct positions among the 256 skeleton points of nodes 2u+1 and 2u+2, those of 2u+1 first. `far_nodes`: each row holds 16 distinct tree nodes.
All inputs are finite; a program needn't handle non-finite values.
Results may differ from a plain program's by a relative error of at most 0.0033.
Values may be sent and summed in bfloat16 or wider, within the bound.
No kernel may reach another device: no remote copies, remote signals or barrier semaphores. Data moves between devices by JAX's collectives and lax.ppermute only.
A program may use at most 128 MiB of HBM per device.

v0:
```python
import math
import jax
import jax.numpy as jnp
from jax import lax
from jax.sharding import PartitionSpec as P

D = 64
NRHS = 32
LEAF = 512
RANK = 128
NEAR = 4
FAR = 16
LEAF_DEV = 2
LAMBDA_RIDGE = 1.0
FULL_PRECISION = lax.Precision.HIGHEST


def kernel_tile(left_points, right_points):
    left_square = jnp.sum(jnp.square(left_points.astype(jnp.float32)), axis=-1)
    right_square = jnp.sum(jnp.square(right_points.astype(jnp.float32)), axis=-1)
    cross_term = jnp.dot(left_points, right_points.T, preferred_element_type=jnp.float32)
    distance = left_square[:, None] + right_square[None, :] - 2.0 * cross_term
    return jnp.exp(distance * (-0.5 / left_points.shape[-1]))


def kernel_batch(left_points, right_points):
    left_wide = left_points.astype(jnp.float32)
    right_wide = right_points.astype(jnp.float32)
    left_square = jnp.sum(left_wide * left_wide, axis=-1)
    right_square = jnp.sum(right_wide * right_wide, axis=-1)
    cross_term = jnp.einsum("bmd,bnd->bmn", left_wide, right_wide, precision=FULL_PRECISION)
    distance = left_square[:, :, None] + right_square[:, None, :] - 2.0 * cross_term
    return jnp.exp(distance * (-0.5 / left_points.shape[-1]))


def far_kernel(own_points, far_points):
    own_square = jnp.sum(jnp.square(own_points.astype(jnp.float32)), axis=-1)
    far_square = jnp.sum(jnp.square(far_points.astype(jnp.float32)), axis=-1)
    cross_term = jnp.einsum(
        "id,frd->fir", own_points, far_points, preferred_element_type=jnp.float32
    )
    distance = own_square[None, :, None] + far_square[:, None, :] - 2.0 * cross_term
    return jnp.exp(distance * (-0.5 / own_points.shape[-1]))


def cholesky_solve(matrix, right_side):
    order = matrix.shape[0]
    indices = jnp.arange(order, dtype=jnp.int32)

    def unit(column):
        return (indices == column).astype(matrix.dtype)

    def factor_step(column, lower):
        pick = unit(column)
        matrix_column = jnp.dot(matrix, pick, precision=FULL_PRECISION)
        lower_row = jnp.dot(pick, lower, precision=FULL_PRECISION)
        remainder = matrix_column - jnp.dot(lower, lower_row, precision=FULL_PRECISION)
        pivot = jnp.sqrt(jnp.sum(remainder * pick))
        new_column = jnp.where(indices >= column, remainder / pivot, jnp.zeros_like(remainder))
        return lower + new_column[:, None] * pick[None, :]

    lower = lax.fori_loop(0, order, factor_step, jnp.zeros_like(matrix))
    diagonal_part = jnp.sum(lower * jnp.eye(order, dtype=matrix.dtype), axis=1)

    def forward_step(column, partial_value):
        pick = unit(column)
        lower_row = jnp.dot(pick, lower, precision=FULL_PRECISION)
        value = (
            jnp.dot(pick, right_side, precision=FULL_PRECISION)
            - jnp.dot(lower_row, partial_value, precision=FULL_PRECISION)
        ) / jnp.sum(diagonal_part * pick)
        return partial_value + pick[:, None] * value[None, :]

    half_solve = lax.fori_loop(0, order, forward_step, jnp.zeros_like(right_side))

    def backward_step(count, partial_value):
        column = order - 1 - count
        pick = unit(column)
        lower_column = jnp.dot(lower, pick, precision=FULL_PRECISION)
        value = (
            jnp.dot(pick, half_solve, precision=FULL_PRECISION)
            - jnp.dot(lower_column, partial_value, precision=FULL_PRECISION)
        ) / jnp.sum(diagonal_part * pick)
        return partial_value + pick[:, None] * value[None, :]

    return lax.fori_loop(0, order, backward_step, jnp.zeros_like(right_side))


def build_levels(level_points, level_weights, upper_skeleton, level_top, level_stop, block_index):
    point_levels = [level_points]
    weight_levels = [level_weights]
    for level_now in range(level_top - 1, level_stop - 1, -1):
        half_count = level_points.shape[0] // 2
        child_points = level_points.reshape(
            half_count, 2 * level_points.shape[1], level_points.shape[2]
        )
        child_weights = level_weights.reshape(
            half_count, 2 * level_weights.shape[1], level_weights.shape[2]
        )
        pick_rows = lax.dynamic_slice_in_dim(
            upper_skeleton, 2**level_now - 1 + block_index * half_count, half_count, 0
        )
        level_points = jax.vmap(
            lambda group_points, group_picks: jnp.take(group_points, group_picks, axis=0)
        )(child_points, pick_rows)
        transfer = kernel_batch(level_points, child_points)
        level_weights = (
            jnp.einsum("bmn,bnc->bmc", transfer, child_weights, precision=FULL_PRECISION)
            / jnp.sum(transfer, axis=2)[:, :, None]
        )
        point_levels.insert(0, level_points)
        weight_levels.insert(0, level_weights)
    return (point_levels, weight_levels)


def split_levels(gathered, group_total):
    per_group = gathered.reshape(group_total, -1, gathered.shape[1], gathered.shape[2])
    pieces_out = []
    width_now = 1
    offset = 0
    while offset < per_group.shape[1]:
        pieces_out.append(
            per_group[:, offset : offset + width_now].reshape(
                group_total * width_now, gathered.shape[1], gathered.shape[2]
            )
        )
        offset = offset + width_now
        width_now = width_now * 2
    return pieces_out


def leaf_image(inputs):
    own_points, near_points, near_values, far_points, far_weights = inputs
    near_tiles = jax.vmap(lambda other_points: kernel_tile(own_points, other_points))(
        near_points
    ).astype(jnp.bfloat16)
    near_part = jnp.einsum(
        "nij,njc->ic", near_tiles, near_values, preferred_element_type=jnp.float32
    )
    far_tiles = far_kernel(own_points, far_points)
    far_part = jnp.einsum("fir,frc->ic", far_tiles, far_weights, precision=FULL_PRECISION)
    return near_part / math.sqrt(own_points.shape[0]) + far_part / far_points.shape[1]


def shards(points, solution, residual, near_leaves, node_skeleton, upper_skeleton, far_nodes):
    gx_count = lax.axis_size("gx")
    gy_count = lax.axis_size("gy")
    row_index = lax.axis_index("gx")
    values_half = residual.astype(jnp.bfloat16)
    flat_points = points.reshape(LEAF_DEV, LEAF * D)
    flat_values = values_half.reshape(LEAF_DEV, LEAF * NRHS)
    request_total = LEAF_DEV * NEAR
    wanted_leaves = near_leaves.reshape(request_total) - row_index * (gy_count * LEAF_DEV)
    piece_points = lax.all_gather(flat_points, "gy", axis=0, tiled=True)
    piece_values = lax.all_gather(flat_values, "gy", axis=0, tiled=True)
    positions = jnp.arange(piece_points.shape[0], dtype=jnp.int32)
    onehot = (wanted_leaves[:, None] == positions[None, :]).astype(jnp.bfloat16)
    got_points = jnp.dot(onehot, piece_points, preferred_element_type=jnp.float32)
    got_values = jnp.dot(onehot, piece_values, preferred_element_type=jnp.float32)
    fetched_points = got_points.astype(jnp.bfloat16)
    fetched_values = got_values.astype(jnp.bfloat16)
    own_points = points.reshape(LEAF_DEV, LEAF, D)
    near_points = jnp.concatenate(
        [own_points[:, None], fetched_points.reshape(LEAF_DEV, NEAR, LEAF, D)], axis=1
    )
    near_values = jnp.concatenate(
        [
            values_half.reshape(LEAF_DEV, 1, LEAF, NRHS),
            fetched_values.reshape(LEAF_DEV, NEAR, LEAF, NRHS),
        ],
        axis=1,
    )
    skeleton_points = jnp.take(points, node_skeleton[0], axis=0)
    node_weights = jnp.dot(
        kernel_tile(skeleton_points, points), residual, precision=FULL_PRECISION
    ) / math.sqrt(points.shape[0])
    depth_total = (gx_count * gy_count).bit_length() - 1
    row_depth = gx_count.bit_length() - 1
    row_points = lax.all_gather(skeleton_points[None], "gy", axis=0, tiled=True)
    row_weights = lax.all_gather(node_weights[None], "gy", axis=0, tiled=True)
    lower_points, lower_weights = build_levels(
        row_points, row_weights, upper_skeleton, depth_total, row_depth, row_index
    )
    every_points = lax.all_gather(jnp.concatenate(lower_points, axis=0), "gx", axis=0, tiled=True)
    every_weights = lax.all_gather(
        jnp.concatenate(lower_weights, axis=0).astype(jnp.bfloat16), "gx", axis=0, tiled=True
    ).astype(jnp.float32)
    middle_points = split_levels(every_points, gx_count)
    middle_weights = split_levels(every_weights, gx_count)
    top_points, top_weights = build_levels(
        middle_points[0], middle_weights[0], upper_skeleton, row_depth, 0, 0
    )
    point_levels = top_points[:-1] + middle_points
    weight_levels = top_weights[:-1] + middle_weights
    tree_points = jnp.concatenate(point_levels, axis=0)
    tree_weights = jnp.concatenate(weight_levels, axis=0)
    far_flat = far_nodes.reshape(-1)
    far_points = jnp.take(tree_points, far_flat, axis=0).reshape(LEAF_DEV, FAR, RANK, D)
    far_weights = jnp.take(tree_weights, far_flat, axis=0).reshape(LEAF_DEV, FAR, RANK, NRHS)
    leaf_terms = lax.map(
        leaf_image, (own_points, near_points, near_values, far_points, far_weights)
    )
    matvec_image = LAMBDA_RIDGE * residual + leaf_terms.reshape(points.shape[0], NRHS)
    gram_matrix, cross_product = lax.psum(
        (
            jnp.dot(matvec_image.T, matvec_image, precision=FULL_PRECISION),
            jnp.dot(matvec_image.T, residual, precision=FULL_PRECISION),
        ),
        ("gx", "gy"),
    )
    step_coeffs = cholesky_solve(gram_matrix, cross_product)
    solution_next = solution + jnp.dot(residual, step_coeffs, precision=FULL_PRECISION)
    residual_next = residual - jnp.dot(matvec_image, step_coeffs, precision=FULL_PRECISION)
    return (solution_next, residual_next, matvec_image)


def solution(mesh):
    placed = (
        P(("gx", "gy"), None),
        P(("gx", "gy"), None),
        P(("gx", "gy"), None),
        P(("gx", "gy"), None),
        P(("gx", "gy"), None),
        P(),
        P(("gx", "gy"), None),
    )
    return jax.shard_map(
        shards,
        mesh=mesh,
        in_specs=placed,
        out_specs=(P(("gx", "gy"), None), P(("gx", "gy"), None), P(("gx", "gy"), None)),
        check_vma=False,
    )
```

profile of v0, /device:TPU:0, one launch (start us, length us, event | category | flops | bytes accessed | tf_op | source)
XLA Modules:
  0.0 403.2 jit_solution(9086683935424094712)
XLA Ops:
  7.2 1.1 copy.103
  8.3 0.9 reshape.473
  13.6 32.8 %all_gather.20 = bf16[8,128,64]{1,2,0:T(8,128)(2,1)S(1)} all-gather(bf16[1,128,64]{1,2,0:T(8,128)(2,1)S(1)} %copy.109), channel_id=1, replica_groups=mesh['gx'=4,'gy'=8] {'gy'}, dimensions={0}, use_global_device_ids=true | all-gather | bytes 147456 | tf_op jit(solution)/shard_map/all_gather | solution.py:179
  46.8 1.0 multiply_reduce_fusion.3
  47.8 0.8 fusion.150
  48.6 0.8 compare_and_fusion
  49.4 3.2 gather_fusion.3
  52.9 1.7 gather_fusion.4
  55.6 1.0 gather_fusion.5
  56.9 9.5 %all_gather.21 = bf16[60,128,64]{1,2,0:T(8,128)(2,1)S(1)} all-gather(bf16[15,128,64]{1,2,0:T(8,128)(2,1)S(1)} %pad_maximum_fusion.2), channel_id=1, replica_groups=mesh['gx'=4,'gy'=8] {'gx'}, dimensions={0}, use_global_device_ids=true | all-gather | bytes 1228800 | tf_op jit(solution)/shard_map/all_gather | solution.py:184
  68.0 30.5 %all-gather = f32[1024,32]{0,1:T(8,128)S(1)} all-gather(f32[128,32]{0,1:T(8,128)S(1)} %convolution_multiply_fusion.6), channel_id=2, replica_groups=mesh['gx'=4,'gy'=8] {'gy'}, dimensions={0}, use_global_device_ids=true | all-gather | bytes 147456 | tf_op jit(solution)/shard_map/all_gather | solution.py:180
  100.6 6.4 %all_gather.23 = bf16[60,128,32]{1,2,0:T(8,128)(2,1)S(1)} all-gather(bf16[15,128,32]{1,2,0:T(8,128)(2,1)S(1)} %pad_maximum_fusion.3), channel_id=1, replica_groups=mesh['gx'=4,'gy'=8] {'gx'}, dimensions={0}, use_global_device_ids=true | all-gather | bytes 614400 | tf_op jit(solution)/shard_map/all_gather | solution.py:185
  108.5 0.9 slice.63
  110.7 1.7 gather_fusion.6
  112.7 1.0 gather_fusion.7
  115.1 0.9 copy.137
  116.0 1.0 copy.138
  117.0 1.1 copy.139
  118.8 1.4 copy_dynamic-update-slice_fusion.1
  120.2 1.5 copy_dynamic-update-slice_fusion
  121.7 1.6 constant_dynamic-update-slice_fusion.2
  125.0 0.9 constant_dynamic-update-slice_fusion
  125.8 1.9 gather_fusion.1
  128.1 31.5 %all-gather.2 = bf16[8,2,16384]{2,1,0:T(2,128)(2,1)S(1)} all-gather(bf16[1,2,16384]{2,1,0:T(2,128)(2,1)S(1)} %reshape.475), channel_id=1, replica_groups=mesh['gx'=4,'gy'=8] {'gy'}, dimensions={0}, use_global_device_ids=true | all-gather | bytes 589824 | tf_op jit(solution)/shard_map/all_gather | solution.py:155
  160.1 0.8 reshape.371
  161.3 0.9 broadcast_select_fusion.1
  162.4 1.5 reshape.474
  164.2 2.1 reshape.368
  166.3 1.5 pad_maximum_fusion
  168.4 16.0 %while.53 = (s32[]{:T(128)}, f32[2,512,32]{1,0,2:T(2,128)}, bf16[2,512,64]{1,2,0:T(8,128)(2,1)S(1)}, bf16[2,5,512,64]{2,3,1,0:T(8,128)(2,1)S(1)}, bf16[2,5,512,3...) while((s32[]{:T(128)}, f32[2,512,32]{1,0,2:T(2,128)}, ...), condition=%wide.region_18.21_spmd, body=%wide.region_14.20_spmd.sunk | while | flops 800304128 | bytes 13847237 | solution.py:200
  169.5 3.5 fusion.244
  173.2 1.9 fusion.245
  177.5 3.5 fusion.244
  181.1 1.9 fusion.245
  184.4 0.9 copy.174
  185.9 39.4 %all-reduce = (f32[32,32]{1,0:T(8,128)S(1)}, f32[32,32]{1,0:T(8,128)S(1)}) all-reduce(f32[32,32]{1,0:T(8,128)S(1)} %fusion.163, f32[32,32]{1,0:T(8,128)S(1)} %fusion.164), channel_id=1, replica_groups=mesh['gx'=4,'gy'=8] {'gx','gy'}, use_global_device_ids=true, to_apply=%region_23.26 | all-reduce | flops 2048 | bytes 16384 | tf_op jit(solution)/shard_map/psum | solution.py:204
  225.2 58.2 %while.56 = (s32[]{:T(128)}, f32[32,32]{1,0:T(8,128)S(1)}, f32[32,32]{1,0:T(8,128)S(1)}, s32[]{:T(128)}, s32[]{:T(128)}) while((s32[]{:T(128)}, f32[32,32]{1,0:T(8,128)S(1)}, f32[32,32]{1,0:T(8,128)S(1)}, s32[]{:T(128)}, s32[]{:T(128)}) %tuple.134), condition=%wide.region_22.25_spmd.clone.clone, body=%wide.region_20.24_spmd.clone.clone.sunk | while | flops 42338 | bytes 21869 | solution.py:62
  225.5 0.8 fusion.270
  227.3 0.8 fusion.270
  229.1 0.8 fusion.270
  231.0 0.8 fusion.270
  232.8 0.8 fusion.270
  238.2 0.8 fusion.270
  272.8 0.8 fusion.270
  283.6 55.3 %while.54 = (s32[]{:T(128)}, f32[32,32]{1,0:T(8,128)S(1)}, f32[32,32]{1,0:T(8,128)S(1)}, f32[32,32]{1,0:T(8,128)S(1)}, f32[32]{0:T(128)S(1)}, /*index=5*/s32[]{:T(128)}, s32[]{:T(128)}) while((s32[]{:T(128)}, f32[32,32]{1,0:T(8,128)S(1)}, f32[32,32]{1,0:T(8,128)S(1)}, f32[32,32]{1,0:T(8,128)S(1)}, f32[32]{0:T(128)S(1)}, ...), condition=%wide.region_27.30_spmd.clone, body=%wide.region_25.29_spmd.clone.sunk | while | flops 41250 | bytes 21744 | solution.py:74
  338.9 55.6 %while.55 = (s32[]{:T(128)}, f32[32,32]{1,0:T(8,128)S(1)}, f32[32,32]{1,0:T(8,128)S(1)}, f32[32,32]{1,0:T(8,128)S(1)}, f32[32]{0:T(128)S(1)}, /*index=5*/s32[]{:T(128)}, s32[]{:T(128)}, s32[]{:T(128)}) while((s32[]{:T(128)}, f32[32,32]{1,0:T(8,128)S(1)}, f32[32,32]{1,0:T(8,128)S(1)}, f32[32,32]{1,0:T(8,128)S(1)}, ...), condition=%wide.region_30.33_spmd.clone, body=%wide.region_28.32_spmd.clone.sunk | while | flops 41251 | bytes 21764 | solution.py:86
  394.4 1.0 convolution_subtract_fusion
  395.4 1.0 fusion.120
  (712 shorter events, 165.5 us)
Async XLA Ops:
  7.2 155.2 %all-gather.5.cloned.1.call-start = ((), (), s32[]{:S(2)}) async-start(), calls=%async_computation | async-start | bytes 1179648 | tf_op jit(solution)/shard_map/all_gather | solution.py:154
  8.3 58.8 %copy-start.2 = (bf16[1024,64]{0,1:T(8,128)(2,1)S(1)}, bf16[1024,64]{0,1:T(8,128)(2,1)}, u32[]{:S(2)}) copy-start(bf16[1024,64]{0,1:T(8,128)(2,1)} %param.19) | copy-start | bytes 393220
  13.4 54.0 %copy-start = (f32[1024,32]{0,1:T(8,128)S(1)}, f32[1024,32]{0,1:T(8,128)}, u32[]{:S(2)}) copy-start(f32[1024,32]{0,1:T(8,128)} %param.21) | copy-start | bytes 393220
  107.0 11.1 %copy-start.11 = (s32[2,16]{1,0:T(2,128)S(1)}, s32[2,16]{1,0:T(2,128)}, u32[]{:S(2)}) copy-start(s32[2,16]{1,0:T(2,128)} %param.25) | copy-start | bytes 388
  112.6 2.2 copy-start.6
  123.4 4.3 %copy-start.10 = (s32[2,4]{1,0:T(2,128)S(1)}, s32[2,4]{1,0:T(2,128)}, u32[]{:S(2)}) copy-start(s32[2,4]{1,0:T(2,128)} %param.22) | copy-start | bytes 100
  125.0 36.2 %copy-start.3 = (bf16[1024,64]{0,1:T(8,128)(2,1)S(1)}, bf16[1024,64]{0,1:T(8,128)(2,1)}, u32[]{:S(2)}) copy-start(bf16[1024,64]{0,1:T(8,128)(2,1)} %param.19) | copy-start | bytes 393220
  168.4 170.5 %copy-start.4 = (f32[32,32]{1,0:T(8,128)S(1)}, f32[32,32]{1,0:T(8,128)}, u32[]{:S(2)}) copy-start(f32[32,32]{1,0:T(8,128)} %custom-call.11) | copy-start | bytes 12292
  168.4 227.0 %copy-start.7 = (f32[1024,32]{0,1:T(8,128)S(1)}, f32[1024,32]{0,1:T(8,128)}, u32[]{:S(2)}) copy-start(f32[1024,32]{0,1:T(8,128)} %param.20) | copy-start | bytes 393220
  168.4 1.1 copy-start.5
  173.1 2.1 copy-start.8
  175.8 0.7 copy-start.9
  176.4 1.0 copy-start.5
  181.0 2.1 copy-start.8
  183.7 0.7 copy-start.9
  185.3 211.0 %copy-start.1 = (f32[1024,32]{0,1:T(8,128)}, f32[1024,32]{0,1:T(8,128)S(1)}, u32[]{:S(2)}) copy-start(f32[1024,32]{0,1:T(8,128)S(1)} %add.319) | copy-start | bytes 393220
Sparse Core Ops, SparseCore 0:
  10.7 43.5 all-gather.4
where the time goes:
time: 405 us; the launch traced here: 403 us
  blocking collectives  150 us (37%)
  matrix products  118 us (29%)
  other arithmetic  58.9 us (15%)
  local copies, waits for them, and re-layouts  38.4 us (9%)
  loops' own time  23.1 us (6%)
  between operations  14.7 us (4%)
    psum x1, blocking collectives, shards(): lax.psum((jnp.dot(matvec_image.T, matvec_image, precision=FULL_PRECISION)...  39.4 us
    all_gather x1, blocking collectives, shards(): row_points = lax.all_gather(skeleton_points[None], 'gy', axis=0, tiled=True)  32.8 us
    all_gather x1, blocking collectives, shards(): piece_values = lax.all_gather(flat_values, 'gy', axis=0, tiled=True)  31.5 us
    all_gather x1, blocking collectives, shards(): row_weights = lax.all_gather(node_weights[None], 'gy', axis=0, tiled=True)  30.5 us
    dot_general x32, matrix products, factor_step(): jnp.dot(lower, lower_row, precision=FULL_PRECISION)  24.9 us
    dot_general x32, matrix products, forward_step(): jnp.dot(lower_row, partial_value, precision=FULL_PRECISION)  24.7 us
    dot_general x32, matrix products, backward_step(): jnp.dot(lower_column, partial_value, precision=FULL_PRECISION)  24.7 us
    another operation x1, loops' own time, cholesky_solve(): lower = lax.fori_loop(0, order, factor_step, jnp.zeros_like(matrix))  22.7 us
  transfers between devices with their start and end apart: 1, of which 0 were waited for; matrix products, arithmetic and copies ran while one was open for 10% of the time, Pallas kernels for 0%

commit v1 on v0

--- a/solution.py
+++ b/solution.py
@@ -151,8 +151,13 @@
     flat_values = values_half.reshape(LEAF_DEV, LEAF * NRHS)
     request_total = LEAF_DEV * NEAR
     wanted_leaves = near_leaves.reshape(request_total) - row_index * (gy_count * LEAF_DEV)
-    piece_points = lax.all_gather(flat_points, "gy", axis=0, tiled=True)
-    piece_values = lax.all_gather(flat_values, "gy", axis=0, tiled=True)
+    piece_points, piece_values = jnp.split(
+        lax.all_gather(
+            jnp.concatenate([flat_points, flat_values], axis=1), "gy", axis=0, tiled=True
+        ),
+        [flat_points.shape[1]],
+        axis=1,
+    )
     positions = jnp.arange(piece_points.shape[0], dtype=jnp.int32)
     onehot = (wanted_leaves[:, None] == positions[None, :]).astype(jnp.bfloat16)
     got_points = jnp.dot(onehot, piece_points, preferred_element_type=jnp.float32)

time: 405 us -> 375 us (0.926)
  blocking collectives: 150 us -> 119 us
  other arithmetic: 58.9 us -> 63 us
    all_gather x1 -> x0, blocking collectives: 31.5 us -> none  [shards(): piece_values = lax.all_gather(flat_values, 'gy', axis=0, tiled=True)]
    unnamed x34 -> x37, local copies, waits for them, and re-layouts: 11.4 us -> 6.1 us
  transfers between devices with their start and end apart: 1 -> 1, of which waited for: 0 -> 0; matrix products, arithmetic and copies ran while one was open for 10% -> 11% of each run, Pallas kernels for 0% -> 0%
where the time goes in v1:
time: 375 us; the launch traced here: 373 us
  blocking collectives  119 us (32%)
  matrix products  118 us (31%)
  other arithmetic  63 us (17%)
  local copies, waits for them, and re-layouts  36.2 us (10%)
  loops' own time  23.1 us (6%)
  between operations  14.6 us (4%)
    psum x1, blocking collectives, shards(): lax.psum((jnp.dot(matvec_image.T, matvec_image, precision=FULL_PRECISION)...  39.3 us
    all_gather x1, blocking collectives, shards(): row_points = lax.all_gather(skeleton_points[None], 'gy', axis=0, tiled=True)  32.7 us
    all_gather x1, blocking collectives, shards(): row_weights = lax.all_gather(node_weights[None], 'gy', axis=0, tiled=True)  30.5 us
    dot_general x32, matrix products, factor_step(): jnp.dot(lower, lower_row, precision=FULL_PRECISION)  24.9 us
    dot_general x32, matrix products, forward_step(): jnp.dot(lower_row, partial_value, precision=FULL_PRECISION)  24.7 us
    dot_general x32, matrix products, backward_step(): jnp.dot(lower_column, partial_value, precision=FULL_PRECISION)  24.7 us
    another operation x1, loops' own time, cholesky_solve(): lower = lax.fori_loop(0, order, factor_step, jnp.zeros_like(matrix))  22.7 us
    reduce_sum x32, other arithmetic, backward_step(): jnp.sum(diagonal_part * pick)  20.2 us
  transfers between devices with their start and end apart: 1, of which 0 were waited for; matrix products, arithmetic and copies ran while one was open for 11% of the time, Pallas kernels for 0%

profile of v1, /device:TPU:0, one launch (start us, length us, event | category | flops | bytes accessed | tf_op | source)
XLA Modules:
  0.0 373.3 jit_solution(5710513791303452102)
XLA Ops:
  7.2 1.1 copy.103
  8.5 0.9 convert_element_type.98
  10.0 0.9 maximum_bitcast_fusion
  15.2 32.7 %all_gather.16 = bf16[8,128,64]{1,2,0:T(8,128)(2,1)S(1)} all-gather(bf16[1,128,64]{1,2,0:T(8,128)(2,1)S(1)} %copy.109), channel_id=1, replica_groups=mesh['gx'=4,'gy'=8] {'gy'}, dimensions={0}, use_global_device_ids=true | all-gather | bytes 147456 | tf_op jit(solution)/shard_map/all_gather | solution.py:184
  48.3 1.0 multiply_reduce_fusion.3
  49.3 0.8 fusion.152
  50.0 1.3 compare_and_fusion
  51.4 3.2 gather_fusion.3
  54.9 1.7 gather_fusion.4
  56.8 1.3 and_bitcast_fusion.1
  58.1 1.0 gather_fusion.5
  59.4 9.6 %all_gather.17 = bf16[60,128,64]{1,2,0:T(8,128)(2,1)S(1)} all-gather(bf16[15,128,64]{1,2,0:T(8,128)(2,1)S(1)} %pad_maximum_fusion.2), channel_id=1, replica_groups=mesh['gx'=4,'gy'=8] {'gx'}, dimensions={0}, use_global_device_ids=true | all-gather | bytes 1228800 | tf_op jit(solution)/shard_map/all_gather | solution.py:189
  71.1 30.5 %all-gather = f32[1024,32]{0,1:T(8,128)S(1)} all-gather(f32[128,32]{0,1:T(8,128)S(1)} %convolution_multiply_fusion.6), channel_id=2, replica_groups=mesh['gx'=4,'gy'=8] {'gy'}, dimensions={0}, use_global_device_ids=true | all-gather | bytes 147456 | tf_op jit(solution)/shard_map/all_gather | solution.py:185
  103.7 6.4 %all_gather.19 = bf16[60,128,32]{1,2,0:T(8,128)(2,1)S(1)} all-gather(bf16[15,128,32]{1,2,0:T(8,128)(2,1)S(1)} %pad_maximum_fusion.3), channel_id=1, replica_groups=mesh['gx'=4,'gy'=8] {'gx'}, dimensions={0}, use_global_device_ids=true | all-gather | bytes 614400 | tf_op jit(solution)/shard_map/all_gather | solution.py:190
  111.6 0.8 slice.63
  114.7 1.7 gather_fusion.6
  117.9 1.6 copy.137
  119.5 1.7 copy.138
  121.2 1.9 copy.139
  123.2 1.0 gather_fusion.7
  126.1 0.9 constant_dynamic-update-slice_fusion.6
  127.0 1.0 constant_dynamic-update-slice_fusion.5
  128.0 1.1 constant_dynamic-update-slice_fusion.4
  129.8 1.0 constant_dynamic-update-slice_fusion.1
  131.7 0.9 broadcast_select_fusion.1
  132.8 1.9 reshape.474
  135.4 2.1 reshape.369
  137.5 1.5 pad_maximum_fusion
  139.6 0.8 reshape.371
  140.8 14.6 %while.53 = (s32[]{:T(128)}, f32[2,512,32]{1,0,2:T(2,128)S(1)}, bf16[2,512,64]{1,2,0:T(8,128)(2,1)S(1)}, bf16[2,5,512,64]{2,3,1,0:T(8,128)(2,1)S(1)}, bf16[2,5,5...) while((s32[]{:T(128)}, f32[2,512,32]{1,0,2:T(2,128)S(1)}, ...), condition=%wide.region_18.21_spmd, body=%wide.region_14.20_spmd.sunk | while | flops 800304128 | bytes 12798605 | solution.py:205
  141.9 3.5 fusion.244
  145.5 1.9 fusion.245
  149.2 3.5 fusion.244
  152.8 1.9 fusion.245
  156.0 39.3 %all-reduce = (f32[32,32]{1,0:T(8,128)S(1)}, f32[32,32]{1,0:T(8,128)S(1)}) all-reduce(f32[32,32]{1,0:T(8,128)S(1)} %fusion.165, f32[32,32]{1,0:T(8,128)S(1)} %fusion.166), channel_id=1, replica_groups=mesh['gx'=4,'gy'=8] {'gx','gy'}, use_global_device_ids=true, to_apply=%region_23.26 | all-reduce | flops 2048 | bytes 16384 | tf_op jit(solution)/shard_map/psum | solution.py:209
  195.3 58.2 %while.56 = (s32[]{:T(128)}, f32[32,32]{1,0:T(8,128)S(1)}, f32[32,32]{1,0:T(8,128)S(1)}, s32[]{:T(128)}, s32[]{:T(128)}) while((s32[]{:T(128)}, f32[32,32]{1,0:T(8,128)S(1)}, f32[32,32]{1,0:T(8,128)S(1)}, s32[]{:T(128)}, s32[]{:T(128)}) %tuple.134), condition=%wide.region_22.25_spmd.clone.clone, body=%wide.region_20.24_spmd.clone.clone.sunk | while | flops 42338 | bytes 21869 | solution.py:62
  195.6 0.8 fusion.270
  197.4 0.8 fusion.270
  199.2 0.8 fusion.270
  201.1 0.8 fusion.270
  202.9 0.8 fusion.270
  204.7 0.8 fusion.270
  212.0 0.8 fusion.270
  246.5 0.8 fusion.270
  253.7 55.2 %while.54 = (s32[]{:T(128)}, f32[32,32]{1,0:T(8,128)S(1)}, f32[32,32]{1,0:T(8,128)S(1)}, f32[32,32]{1,0:T(8,128)S(1)}, f32[32]{0:T(128)S(1)}, /*index=5*/s32[]{:T(128)}, s32[]{:T(128)}) while((s32[]{:T(128)}, f32[32,32]{1,0:T(8,128)S(1)}, f32[32,32]{1,0:T(8,128)S(1)}, f32[32,32]{1,0:T(8,128)S(1)}, f32[32]{0:T(128)S(1)}, ...), condition=%wide.region_27.30_spmd.clone, body=%wide.region_25.29_spmd.clone.sunk | while | flops 41250 | bytes 21744 | solution.py:74
  308.9 55.6 %while.55 = (s32[]{:T(128)}, f32[32,32]{1,0:T(8,128)S(1)}, f32[32,32]{1,0:T(8,128)S(1)}, f32[32,32]{1,0:T(8,128)S(1)}, f32[32]{0:T(128)S(1)}, /*index=5*/s32[]{:T(128)}, s32[]{:T(128)}, s32[]{:T(128)}) while((s32[]{:T(128)}, f32[32,32]{1,0:T(8,128)S(1)}, f32[32,32]{1,0:T(8,128)S(1)}, f32[32,32]{1,0:T(8,128)S(1)}, ...), condition=%wide.region_30.33_spmd.clone, body=%wide.region_28.32_spmd.clone.sunk | while | flops 41251 | bytes 21764 | solution.py:86
  364.5 1.0 convolution_subtract_fusion
  365.5 1.0 fusion.120
  (709 shorter events, 165.2 us)
Async XLA Ops:
  7.2 125.6 %all-gather.4.cloned.1.call-start = ((), (), s32[]{:S(2)}) async-start(), calls=%async_computation | async-start | bytes 1769472 | tf_op jit(solution)/shard_map/all_gather | solution.py:155
  9.9 60.2 %copy-start.2 = (bf16[1024,64]{0,1:T(8,128)(2,1)S(1)}, bf16[1024,64]{0,1:T(8,128)(2,1)}, u32[]{:S(2)}) copy-start(bf16[1024,64]{0,1:T(8,128)(2,1)} %param.19) | copy-start | bytes 393220
  15.0 55.5 %copy-start = (f32[1024,32]{0,1:T(8,128)S(1)}, f32[1024,32]{0,1:T(8,128)}, u32[]{:S(2)}) copy-start(f32[1024,32]{0,1:T(8,128)} %param.21) | copy-start | bytes 393220
  110.1 13.0 %copy-start.11 = (s32[2,16]{1,0:T(2,128)S(1)}, s32[2,16]{1,0:T(2,128)}, u32[]{:S(2)}) copy-start(s32[2,16]{1,0:T(2,128)} %param.25) | copy-start | bytes 388
  110.1 14.0 %copy-start.9 = (pred[128]{0:T(512)(128)(4,1)S(1)}, pred[128]{0:T(512)(128)(4,1)}, u32[]{:S(2)}) copy-start(pred[128]{0:T(512)(128)(4,1)} %get-tuple-element.489) | copy-start | bytes 388
  123.1 6.7 %copy-start.3 = (bf16[4,2,128,64]{2,3,1,0:T(8,128)(2,1)S(1)}, bf16[4,2,128,64]{2,3,1,0:T(8,128)(2,1)}, u32[]{:S(2)}) copy-start(bf16[4,2,128,64]{2,3,1,0:T(8,128)(2,1)} %slice.56) | copy-start | bytes 393220
  125.3 4.4 %copy-start.8 = (bf16[1,128,64]{1,2,0:T(8,128)(2,1)S(1)}, bf16[1,128,64]{1,2,0:T(8,128)(2,1)}, u32[]{:S(2)}) copy-start(bf16[1,128,64]{1,2,0:T(8,128)(2,1)} %copy.120) | copy-start | bytes 49156
  129.1 2.5 copy-start.10
  129.1 2.6 copy-start.5
  129.1 2.6 copy-start.12
  137.5 3.3 copy-start.7
  140.8 224.7 %copy-start.6 = (f32[1024,32]{0,1:T(8,128)S(1)}, f32[1024,32]{0,1:T(8,128)}, u32[]{:S(2)}) copy-start(f32[1024,32]{0,1:T(8,128)} %param.20) | copy-start | bytes 393220
  140.8 1.1 copy-start.4
  148.1 1.0 copy-start.4
  155.5 211.0 %copy-start.1 = (f32[1024,32]{0,1:T(8,128)}, f32[1024,32]{0,1:T(8,128)S(1)}, u32[]{:S(2)}) copy-start(f32[1024,32]{0,1:T(8,128)S(1)} %add.319) | copy-start | bytes 393220
Sparse Core Ops, SparseCore 0:
  11.0 47.4 all-gather.3
